TPU v7x, 256 devices: a whole 4x4x8 slice. The times are simulated.
256 devices in a mesh: seq: 32 (over z_lo, x, core), cam: 4 (over y), tp: 2 (over z_hi).
Axes of the slice: x: 4, y: 4, z: 8 (z_hi: 2, z_lo: 4; z = z_hi * 4 + z_lo), core: 2. Of those that a mesh axis runs over, the one named last changes fastest.
Arguments:
- pixel_feature: bfloat16 [32768, 2048], P(('seq', 'cam'), 'tp'), may hold values from -6 to 6
- depth_score: float32 [32768, 59], P(('seq', 'cam')), may hold values from 0.05 to 5
- depth_bin: int32 [32768, 4], P(('seq', 'cam')), may hold values from 0 to 58
- cell_owner: int32 [131072, 1], P(('seq', 'cam')), may hold values from 0 to 31; in each aligned block of 1024 rows (0 to 1023, 1024 to 2047, ...) at most 64 rows name the same one
- cell_local: int32 [32768, 4], P(('seq', 'cam')), may hold values from 0 to 7
- frame_keep: int32 [64], replicated, may hold values 0 or 1
- norm_gain: float32 [2048], P('tp'), may hold values from 0.1 to 1.9
- w_query: bfloat16 [2048, 2048], P(None, ('cam', 'tp')), may hold values from -1.5 to 1.5
- w_key: bfloat16 [2048, 2048], P(None, ('cam', 'tp')), may hold values from -0.375 to 0.375
- w_value: bfloat16 [2048, 2048], P(None, ('cam', 'tp')), may hold values from -0.125 to 0.125
Outputs:
- attended: bfloat16 [16384, 2048], P('seq', ('cam', 'tp'))
Inputs may be any that keep to these rules, and one draw needn't show every extreme that they name: `cell_owner`: among the 1024 points of one index of seq and cam (aligned blocks of rows), no owner is named more than 64 times, a bound that some block reaches.
All inputs are finite; a program needn't handle non-finite values.
Results may differ from a plain program's by a relative error of at most 0.028.
The roundings to bfloat16 on the way count: a program that leaves them out, or rounds other values in their place, can miss the bound.
Values may be sent and summed in bfloat16 or wider, within the bound.
A program may use at most 64 MiB of HBM per device.

v0:
```python
import jax
import jax.numpy as jnp
from jax import lax
from jax.sharding import PartitionSpec as P

D = 2048
HD = 128
CELL_DEV = 8
epsilon = 1e-05
block_rows = 512


def attend(state, query, query_start, keys, values, key_start, frame_keep):
    frames = frame_keep.shape[0]
    frame_query = (query_start + jnp.arange(query.shape[0], dtype=jnp.int32)) % frames
    frame_key = (key_start + jnp.arange(keys.shape[0], dtype=jnp.int32)) % frames
    frame_list = jnp.arange(frames, dtype=jnp.int32)
    kept = jnp.sum(
        jnp.where(frame_key[:, None] == frame_list[None, :], frame_keep[None, :], 0), axis=1
    )
    allowed = (frame_key[None, :] <= frame_query[:, None]) & (
        (kept[None, :] > 0) | (frame_key[None, :] == frame_query[:, None])
    )
    scores = jnp.einsum("qhd,khd->hqk", query, keys, preferred_element_type=jnp.float32) * (
        1.0 / HD**0.5
    )
    accum, peak, total = state
    new_peak = jnp.maximum(peak, jnp.max(jnp.where(allowed[None], scores, -1e30), axis=2))
    factor = jnp.exp(peak - new_peak)
    expo = jnp.where(allowed[None], jnp.exp(scores - new_peak[:, :, None]), 0.0)
    mixed = jnp.einsum(
        "hqk,khd->hqd", expo.astype(jnp.bfloat16), values, preferred_element_type=jnp.float32
    )
    return (accum * factor[:, :, None] + mixed, new_peak, total * factor + jnp.sum(expo, axis=2))


def local(
    pixel_feature,
    depth_score,
    depth_bin,
    cell_owner,
    cell_local,
    frame_keep,
    norm_gain,
    w_query,
    w_key,
    w_value,
):
    pixels, half = pixel_feature.shape
    keep_count = depth_bin.shape[1]
    points = pixels * keep_count
    seq_count = lax.axis_size("seq")
    seq_index = lax.axis_index("seq")
    frames = frame_keep.shape[0]
    frames_dev = frames // seq_count
    tokens_dev = CELL_DEV * frames
    capacity = 2 * points // seq_count
    prob = depth_score / jnp.sum(depth_score, axis=1, keepdims=True)
    bins = jnp.arange(depth_score.shape[1], dtype=jnp.int32)
    picked = jnp.sum(
        jnp.where(depth_bin[:, :, None] == bins[None, None, :], prob[:, None, :], 0.0), axis=2
    )
    weight = picked.astype(jnp.bfloat16)
    point_index = jnp.arange(points, dtype=jnp.int32).reshape(pixels, keep_count)
    local_frame = point_index // (points // frames_dev)
    owner = cell_owner[:, 0].reshape(pixels, keep_count)
    owner_flat = owner.reshape(points)
    hits = (owner_flat[:, None] == jnp.arange(seq_count, dtype=jnp.int32)[None, :]).astype(
        jnp.int32
    )
    rank = jnp.sum(jnp.cumsum(hits, axis=0) * hits, axis=1) - 1
    slot = owner_flat * capacity + rank
    point_rows = jnp.repeat(pixel_feature, keep_count, axis=0)
    send_rows = jnp.zeros((seq_count * capacity, half), jnp.bfloat16).at[slot].set(point_rows)
    send_rows = send_rows.reshape(seq_count, capacity, half)
    frame_global = seq_index * frames_dev + local_frame
    describe = jnp.stack(
        [
            weight.reshape(points),
            cell_local.reshape(points).astype(jnp.bfloat16),
            frame_global.reshape(points).astype(jnp.bfloat16),
        ],
        axis=0,
    )
    send_meta = jnp.zeros((3, seq_count * capacity), jnp.bfloat16).at[:, slot].set(describe)
    send_meta = send_meta.reshape(3, seq_count, capacity).transpose(1, 0, 2)
    got_rows, got_meta = (
        lax.all_to_all(send_rows, "seq", split_axis=0, concat_axis=0, tiled=True),
        lax.all_to_all(send_meta, "seq", split_axis=0, concat_axis=0, tiled=True),
    )
    target = (
        got_meta[:, 1, :].astype(jnp.float32) * frames + got_meta[:, 2, :].astype(jnp.float32)
    ).reshape(-1)
    token_ids = jnp.arange(tokens_dev, dtype=jnp.float32)
    mixing = jnp.where(
        token_ids[:, None] == target[None, :], got_meta[:, 0, :].reshape(-1)[None, :], 0
    )
    pooled = jnp.dot(mixing, got_rows.reshape(-1, half), preferred_element_type=jnp.float32)
    bev = lax.psum(pooled, "cam")
    squares = lax.psum(jnp.sum(bev * bev, axis=1), "tp")
    normed = (bev * lax.rsqrt(squares[:, None] / D + epsilon) * norm_gain[None, :]).astype(
        jnp.bfloat16
    )
    width = w_query.shape[1]
    heads_dev = width // HD
    piece = lax.all_gather(normed, "tp", axis=1, tiled=True)
    query_sum = jnp.dot(piece, w_query, preferred_element_type=jnp.float32)
    key_sum = jnp.dot(piece, w_key, preferred_element_type=jnp.float32)
    value_sum = jnp.dot(piece, w_value, preferred_element_type=jnp.float32)
    query = query_sum.astype(jnp.bfloat16).reshape(tokens_dev, heads_dev, HD)
    keys = key_sum.astype(jnp.bfloat16).reshape(tokens_dev, heads_dev, HD)
    values = value_sum.astype(jnp.bfloat16).reshape(tokens_dev, heads_dev, HD)
    query_start = seq_index * tokens_dev
    start_state = (
        jnp.zeros((heads_dev, tokens_dev, HD), jnp.float32),
        jnp.full((heads_dev, tokens_dev), -1e30, jnp.float32),
        jnp.zeros((heads_dev, tokens_dev), jnp.float32),
    )
    piece_keys = lax.all_gather(keys, "seq", axis=0, tiled=True)
    piece_values = lax.all_gather(values, "seq", axis=0, tiled=True)
    count = piece_keys.shape[0]

    def one_block(index, inner):
        block_keys = lax.dynamic_slice_in_dim(piece_keys, index * block_rows, block_rows, 0)
        block_values = lax.dynamic_slice_in_dim(piece_values, index * block_rows, block_rows, 0)
        return attend(
            inner, query, query_start, block_keys, block_values, index * block_rows, frame_keep
        )

    accum, peak, total = lax.fori_loop(0, count // block_rows, one_block, start_state)
    result = accum / total[:, :, None]
    return result.transpose(1, 0, 2).reshape(tokens_dev, width).astype(jnp.bfloat16)


def solution(mesh):
    return jax.shard_map(
        local,
        mesh=mesh,
        in_specs=(
            P(("seq", "cam"), "tp"),
            P(("seq", "cam"), None),
            P(("seq", "cam"), None),
            P(("seq", "cam"), None),
            P(("seq", "cam"), None),
            P(),
            P("tp"),
            P(None, ("cam", "tp")),
            P(None, ("cam", "tp")),
            P(None, ("cam", "tp")),
        ),
        out_specs=P("seq", ("cam", "tp")),
        check_vma=False,
    )
```

profile of v0, /device:TPU:1, one launch (start us, length us, event | category | flops | bytes accessed | tf_op | source)
XLA Modules:
  0.0 587.0 jit_solution(16973022452448787255)
XLA Ops:
  11.1 9.0 %reduce-window.6 = s32[32,8,128]{2,1,0:T(8,128)S(1)} reduce-window(s32[32,8,128]{2,1,0:T(8,128)S(1)} %fusion.34, s32[]{:T(128)} %constant.143.clone.1), window={size=1x1x128 pad=0_0x0_0x127_0}, to_apply=%region_0.0 | reduce-window | flops 4161536 | bytes 262148 | tf_op jit(solution)/shard_map/reduce-window
  22.4 3.3 scatter_custom_fusion
  26.7 10.0 %all-to-all-start = ((bf16[32,3,64]{2,1,0:T(4,128)(2,1)}), bf16[32,3,64]{2,1,0:T(4,128)(2,1)S(1)}, u32[]{:S(2)}, u32[]{:S(2)}) async-start(bf16[32,3,64]{2,1,0:T(4,128)(2,1)} %bitcast.8), calls=%async_computation | async-start | bytes 65536 | tf_op jit(solution)/shard_map/all_to_all | solution.py:89
  38.4 2.1 reshape.333
  40.4 8.6 %scatter_custom_fusion.1 = bf16[2048,1024]{1,0:T(8,128)(2,1)} fusion(s32[1024]{0:T(1024)S(1)} %bitcast.76, bf16[1024,1024]{1,0:T(8,128)(2,1)} %reshape.333, bf16[]{:T(256)} %constant.146.clone.1), kind=kCustom, calls=%fused_computation.44 | custom fusion | bytes 4194816 | tf_op jit(solution)/shard_map/scatter | solution.py:74
  49.0 7.8 %all-to-all-start.1 = ((bf16[32,64,1024]{2,1,0:T(8,128)(2,1)}), bf16[32,64,1024]{2,1,0:T(8,128)(2,1)}, u32[]{:S(2)}, u32[]{:S(2)}) async-start(bf16[32,64,1024]{2,1,0:T(8,128)(2,1)} %bitcast.65), calls=%async_computation.1 | async-start | bytes 8388608 | tf_op jit(solution)/shard_map/all_to_all | solution.py:88
  57.2 92.7 %all-to-all-done.1 = bf16[32,64,1024]{2,1,0:T(8,128)(2,1)} async-done(((bf16[32,64,1024]{2,1,0:T(8,128)(2,1)}), bf16[32,64,1024]{2,1,0:T(8,128)(2,1)}, u32[]{:S(2)}, u32[]{:S(2)}) %all-to-all-start.1) | async-done | bytes 4194336 | tf_op jit(solution)/shard_map/all_to_all | solution.py:88
  149.9 5.9 fusion.22
  155.8 64.2 %all-reduce.2.cloned.1.call-done = f32[512,1024]{1,0:T(8,128)} async-done(((f32[512,1024]{1,0:T(8,128)}), f32[512,1024]{1,0:T(8,128)}) %all-reduce.2.cloned.1.call-update) | async-done | bytes 2097168 | tf_op jit(solution)/shard_map/psum | solution.py:99
  221.9 7.8 %psum.15 = f32[512]{0:T(512)S(1)} all-reduce(f32[512]{0:T(512)S(1)} %multiply_reduce_fusion), channel_id=1, replica_groups=mesh['seq'=32,'cam'=4,'tp'=2] {'tp'}, use_global_device_ids=true, to_apply=%region_9.10 | all-reduce | flops 512 | bytes 4096 | tf_op jit(solution)/shard_map/psum | solution.py:100
  231.2 65.9 %all-gather.4.cloned.1.call-done = bf16[512,2048]{1,0:T(8,128)(2,1)} async-done(((bf16[512,1024]{1,0:T(8,128)(2,1)}), bf16[512,2048]{1,0:T(8,128)(2,1)}) %all-gather.4.cloned.1.call-update) | async-done | bytes 2097168 | tf_op jit(solution)/shard_map/all_gather | solution.py:106
  297.2 2.5 convolution_convert_fusion
  300.6 2.0 convolution_convert_fusion.2
  303.5 2.6 convolution_convert_fusion.1
  306.3 59.7 %all-gather.8.cloned.1.call-done = bf16[16384,2,128]{2,0,1:T(8,128)(2,1)} async-done(((bf16[512,2,128]{2,0,1:T(8,128)(2,1)}), bf16[16384,2,128]{2,0,1:T(8,128)(2,1)}) %all-gather.8.cloned.1.call-update) | async-done | bytes 8388624 | tf_op jit(solution)/shard_map/all_gather | solution.py:120
  366.0 69.0 %all-gather.6.cloned.1.call-done = bf16[16384,2,128]{2,0,1:T(8,128)(2,1)} async-done(((bf16[512,2,128]{2,0,1:T(8,128)(2,1)}), bf16[16384,2,128]{2,0,1:T(8,128)(2,1)}) %all-gather.6.cloned.1.call-update) | async-done | bytes 8388624 | tf_op jit(solution)/shard_map/all_gather | solution.py:119
  435.0 144.5 %while.20 = (s32[]{:T(128)}, f32[2,512,128]{2,1,0:T(8,128)S(1)}, f32[2,512]{1,0:T(2,128)S(1)}, f32[2,512]{1,0:T(2,128)S(1)}, s32[]{:T(128)}, /*index=5*/s32[64]{...) while((s32[]{:T(128)}, f32[2,512,128]{2,1,0:T(8,128)S(1)}, ...), condition=%wide.region_14.15_spmd.clone, body=%wide.region_10.14_spmd.clone.sunk | while | flops 275760128 | bytes 9256399 | solution.py:130
  437.5 2.0 convolution_add_fusion.2
  442.0 2.0 convolution_add_fusion.2
  446.5 2.0 convolution_add_fusion.2
  451.0 2.0 convolution_add_fusion.2
  455.5 2.0 convolution_add_fusion.2
  460.1 2.0 convolution_add_fusion.2
  464.6 2.0 convolution_add_fusion.2
  469.1 2.0 convolution_add_fusion.2
  473.6 2.0 convolution_add_fusion.2
  482.7 2.0 convolution_add_fusion.2
  487.2 2.0 convolution_add_fusion.2
  491.7 2.0 convolution_add_fusion.2
  500.7 2.0 convolution_add_fusion.2
  505.2 2.0 convolution_add_fusion.2
  509.8 2.0 convolution_add_fusion.2
  (363 shorter events, 129.2 us)
Async XLA Ops:
  6.5 290.6 %copy-start = (bf16[2048,256]{1,0:T(8,128)(2,1)S(1)}, bf16[2048,256]{1,0:T(8,128)(2,1)}, u32[]{:S(2)}) copy-start(bf16[2048,256]{1,0:T(8,128)(2,1)} %param.21) | copy-start | bytes 3145732
  26.7 22.4 %all-to-all-start = ((bf16[32,3,64]{2,1,0:T(4,128)(2,1)}), bf16[32,3,64]{2,1,0:T(4,128)(2,1)S(1)}, u32[]{:S(2)}, u32[]{:S(2)}) async-start(bf16[32,3,64]{2,1,0:T(4,128)(2,1)} %bitcast.8), calls=%async_computation | async-start | bytes 65536 | tf_op jit(solution)/shard_map/all_to_all | solution.py:89
  49.0 100.9 %all-to-all-start.1 = ((bf16[32,64,1024]{2,1,0:T(8,128)(2,1)}), bf16[32,64,1024]{2,1,0:T(8,128)(2,1)}, u32[]{:S(2)}, u32[]{:S(2)}) async-start(bf16[32,64,1024]{2,1,0:T(8,128)(2,1)} %bitcast.65), calls=%async_computation.1 | async-start | bytes 8388608 | tf_op jit(solution)/shard_map/all_to_all | solution.py:88
  56.8 163.2 %all-reduce.2.cloned.1.call-start = ((), (), s32[]{:S(2)}) async-start(), calls=%async_computation.2 | async-start | bytes 4194304 | tf_op jit(solution)/shard_map/psum | solution.py:99
  155.7 74.0 %copy-start.3 = (f32[1024]{0:T(1024)S(1)}, f32[1024]{0:T(1024)}, u32[]{:S(2)}) copy-start(f32[1024]{0:T(1024)} %param.18) | copy-start | bytes 12292
  155.8 141.4 %all-gather.4.cloned.1.call-start = ((), (), s32[]{:S(2)}) async-start(), calls=%async_computation.3 | async-start | bytes 3145728 | tf_op jit(solution)/shard_map/all_gather | solution.py:106
  220.0 9.7 %copy-start.1 = (f32[512,1024]{1,0:T(8,128)S(1)}, f32[512,1024]{1,0:T(8,128)}, u32[]{:S(2)}) copy-start(f32[512,1024]{1,0:T(8,128)} %all-reduce.2.cloned.1.call-done) | copy-start | bytes 6291460
  231.0 135.0 %all-gather.8.cloned.1.call-start = ((), (), s32[]{:S(2)}) async-start(), calls=%async_computation.5 | async-start | bytes 8650752 | tf_op jit(solution)/shard_map/all_gather | solution.py:120
  297.2 3.4 copy-start.4
  300.5 134.4 %all-gather.6.cloned.1.call-start = ((), (), s32[]{:S(2)}) async-start(), calls=%async_computation.4 | async-start | bytes 8650752 | tf_op jit(solution)/shard_map/all_gather | solution.py:119
  303.5 131.5 %copy-start.2 = (s32[64]{0:T(128)S(1)}, s32[64]{0:T(128)}, u32[]{:S(2)}) copy-start(s32[64]{0:T(128)} %param.17) | copy-start | bytes 772
Sparse Core Ops, SparseCore 0:
  155.9 64.0 all-reduce.1
  231.1 66.0 all-gather.3
  300.7 65.2 all-gather.7
  367.7 67.1 all-gather.5
where the time goes:
time: 590 us; the launch traced here: 587 us
  waiting for transfers between devices  352 us (60%)
  matrix products  124 us (21%)
  other arithmetic  50.4 us (9%)
  local copies, waits for them, and re-layouts  19.9 us (3%)
  starting transfers between devices  18.1 us (3%)
  between operations  13.3 us (2%)
  blocking collectives  7.76 us (1%)
    all_to_all x1, waiting for transfers between devices, local(): lax.all_to_all(send_rows, 'seq', split_axis=0, concat_axis=0, tiled=True)  92.7 us
    all_gather x1, waiting for transfers between devices, local(): piece_keys = lax.all_gather(keys, 'seq', axis=0, tiled=True)  69 us
    all_gather x1, waiting for transfers between devices, local(): piece = lax.all_gather(normed, 'tp', axis=1, tiled=True)  65.9 us
    psum x1, waiting for transfers between devices, local(): bev = lax.psum(pooled, 'cam')  64.2 us
    dot_general x32, matrix products, attend(): jnp.einsum('hqk,khd->hqd', expo.astype(jnp.bfloat16), values, preferred_e...  62.6 us
    all_gather x1, waiting for transfers between devices, local(): piece_values = lax.all_gather(values, 'seq', axis=0, tiled=True)  59.7 us
    dot_general x32, matrix products, attend(): jnp.einsum('qhd,khd->hqk', query, keys, preferred_element_type=jnp.float32)  48.2 us
    reduce_sum x32, other arithmetic, attend(): jnp.sum(expo, axis=2)  15.9 us
  transfers between devices with their start and end apart: 6, of which 5 were waited for; matrix products, arithmetic and copies ran while one was open for 3% of the time, Pallas kernels for 0%

commit v1 on v0

--- a/solution.py
+++ b/solution.py
@@ -117,7 +117,15 @@
         jnp.zeros((heads_dev, tokens_dev), jnp.float32),
     )
     piece_keys = lax.all_gather(keys, "seq", axis=0, tiled=True)
-    piece_values = lax.all_gather(values, "seq", axis=0, tiled=True)
+    piece_values = jnp.concatenate(
+        lax.all_to_all(
+            jnp.stack(lax.axis_size("seq") * [values], 0),
+            axis_name="seq",
+            split_axis=0,
+            concat_axis=0,
+        ),
+        0,
+    )
     count = piece_keys.shape[0]
 
     def one_block(index, inner):

time: 590 us -> 745 us (1.26)
  waiting for transfers between devices: 352 us -> 443 us
  local copies, waits for them, and re-layouts: 19.9 us -> 75.6 us
    all_to_all x0 -> x1, waiting for transfers between devices: none -> 220 us  [local(): lax.all_to_all(jnp.stack(lax.axis_size('seq') * [values], 0), axis_name='...]
    all_gather x1, waiting for transfers between devices: 69 us -> 0.01 us  [local(): piece_keys = lax.all_gather(keys, 'seq', axis=0, tiled=True)]
    all_gather x1 -> x0, waiting for transfers between devices: 59.7 us -> none  [local(): piece_values = lax.all_gather(values, 'seq', axis=0, tiled=True)]
    while x32 -> x160, local copies, waits for them, and re-layouts: 0.08 us -> 42.9 us
    all_to_all x0 -> x1, local copies, waits for them, and re-layouts: none -> 7.59 us  [local(): lax.all_to_all(jnp.stack(lax.axis_size('seq') * [values], 0), axis_name='...]
  transfers between devices with their start and end apart: 6 -> 6, of which waited for: 5 -> 4; matrix products, arithmetic and copies ran while one was open for 3% -> 3% of each run, Pallas kernels for 0% -> 0%
where the time goes in v1:
time: 745 us; the launch traced here: 741 us
  waiting for transfers between devices  443 us (59%)
  matrix products  124 us (17%)
  local copies, waits for them, and re-layouts  75.6 us (10%)
  other arithmetic  51.3 us (7%)
  starting transfers between devices  23.4 us (3%)
  between operations  13.3 us (2%)
  blocking collectives  7.94 us (1%)
    all_to_all x1, waiting for transfers between devices, local(): lax.all_to_all(jnp.stack(lax.axis_size('seq') * [values], 0), axis_name='...  220 us
    all_to_all x1, waiting for transfers between devices, local(): lax.all_to_all(send_rows, 'seq', split_axis=0, concat_axis=0, tiled=True)  92.7 us
    all_gather x1, waiting for transfers between devices, local(): piece = lax.all_gather(normed, 'tp', axis=1, tiled=True)  66.2 us
    psum x1, waiting for transfers between devices, local(): bev = lax.psum(pooled, 'cam')  64.2 us
    dot_general x32, matrix products, attend(): jnp.einsum('hqk,khd->hqd', expo.astype(jnp.bfloat16), values, preferred_e...  61.4 us
    dot_general x32, matrix products, attend(): jnp.einsum('qhd,khd->hqk', query, keys, preferred_element_type=jnp.float32)  50.7 us
    while x160, local copies, waits for them, and re-layouts  42.9 us
    reduce_sum x32, other arithmetic, attend(): jnp.sum(expo, axis=2)  15.9 us
  transfers between devices with their start and end apart: 6, of which 4 were waited for; matrix products, arithmetic and copies ran while one was open for 3% of the time, Pallas kernels for 0%

profile of v1, /device:TPU:1, one launch (start us, length us, event | category | flops | bytes accessed | tf_op | source)
XLA Modules:
  0.0 741.0 jit_solution(11963761777214676723)
XLA Ops:
  7.3 9.0 %reduce-window.6 = s32[32,8,128]{2,1,0:T(8,128)S(1)} reduce-window(s32[32,8,128]{2,1,0:T(8,128)S(1)} %fusion.34, s32[]{:T(128)} %constant.143.clone.1), window={size=1x1x128 pad=0_0x0_0x127_0}, to_apply=%region_0.0 | reduce-window | flops 4161536 | bytes 262148 | tf_op jit(solution)/shard_map/reduce-window
  22.4 3.3 scatter_custom_fusion
  26.6 10.0 %all-to-all-start = ((bf16[32,3,64]{2,1,0:T(4,128)(2,1)}), bf16[32,3,64]{2,1,0:T(4,128)(2,1)S(1)}, u32[]{:S(2)}, u32[]{:S(2)}) async-start(bf16[32,3,64]{2,1,0:T(4,128)(2,1)} %bitcast.8), calls=%async_computation | async-start | bytes 65536 | tf_op jit(solution)/shard_map/all_to_all | solution.py:89
  38.4 2.1 reshape.335
  40.4 8.6 %scatter_custom_fusion.1 = bf16[2048,1024]{1,0:T(8,128)(2,1)} fusion(s32[1024]{0:T(1024)S(1)} %bitcast.76, bf16[1024,1024]{1,0:T(8,128)(2,1)} %reshape.335, bf16[]{:T(256)} %constant.146.clone.1), kind=kCustom, calls=%fused_computation.44 | custom fusion | bytes 4194816 | tf_op jit(solution)/shard_map/scatter | solution.py:74
  49.0 7.8 %all-to-all-start.1 = ((bf16[32,64,1024]{2,1,0:T(8,128)(2,1)}), bf16[32,64,1024]{2,1,0:T(8,128)(2,1)}, u32[]{:S(2)}, u32[]{:S(2)}) async-start(bf16[32,64,1024]{2,1,0:T(8,128)(2,1)} %bitcast.64), calls=%async_computation.1 | async-start | bytes 8388608 | tf_op jit(solution)/shard_map/all_to_all | solution.py:88
  57.2 92.7 %all-to-all-done.1 = bf16[32,64,1024]{2,1,0:T(8,128)(2,1)} async-done(((bf16[32,64,1024]{2,1,0:T(8,128)(2,1)}), bf16[32,64,1024]{2,1,0:T(8,128)(2,1)}, u32[]{:S(2)}, u32[]{:S(2)}) %all-to-all-start.1) | async-done | bytes 4194336 | tf_op jit(solution)/shard_map/all_to_all | solution.py:88
  149.9 5.9 fusion.22
  155.8 64.2 %all-reduce.2.cloned.1.call-done = f32[512,1024]{1,0:T(8,128)} async-done(((f32[512,1024]{1,0:T(8,128)}), f32[512,1024]{1,0:T(8,128)}) %all-reduce.2.cloned.1.call-update) | async-done | bytes 2097168 | tf_op jit(solution)/shard_map/psum | solution.py:99
  220.0 2.0 multiply_reduce_fusion
  221.9 7.9 %psum.15 = f32[512]{0:T(512)S(1)} all-reduce(f32[512]{0:T(512)S(1)} %multiply_reduce_fusion), channel_id=1, replica_groups=mesh['seq'=32,'cam'=4,'tp'=2] {'tp'}, use_global_device_ids=true, to_apply=%region_9.10 | all-reduce | flops 512 | bytes 4096 | tf_op jit(solution)/shard_map/psum | solution.py:100
  231.2 66.2 %all-gather.3.cloned.1.call-done = bf16[512,2048]{1,0:T(8,128)(2,1)} async-done(((bf16[512,1024]{1,0:T(8,128)(2,1)}), bf16[512,2048]{1,0:T(8,128)(2,1)}) %all-gather.3.cloned.1.call-update) | async-done | bytes 2097168 | tf_op jit(solution)/shard_map/all_gather | solution.py:106
  297.3 2.3 convolution_convert_fusion
  299.9 5.2 stack.9
  305.1 5.5 all-to-all-start.2
  310.7 2.0 convolution_convert_fusion.2
  313.6 2.0 convolution_convert_fusion.1
  316.4 220.1 %all-to-all-done.2 = bf16[32,512,2,128]{3,1,2,0:T(8,128)(2,1)} async-done(((bf16[32,512,2,128]{3,1,2,0:T(8,128)(2,1)}), bf16[32,512,2,128]{3,1,2,0:T(8,128)(2,1)}, u32[]{:S(2)}, u32[]{:S(2)}) %all-to-all-start.2) | async-done | bytes 8388640 | tf_op jit(solution)/shard_map/all_to_all | solution.py:121
  536.5 7.6 %copy.64 = bf16[32,512,2,128]{3,1,0,2:T(8,128)(2,1)} copy(bf16[32,512,2,128]{3,1,2,0:T(8,128)(2,1)} %all-to-all-done.2) | data formatting | bytes 16777216 | tf_op jit(solution)/shard_map/all_to_all | solution.py:121
  544.1 188.5 %while.20 = (s32[]{:T(128)}, f32[2,512,128]{2,1,0:T(8,128)}, f32[2,512]{1,0:T(2,128)S(1)}, f32[2,512]{1,0:T(2,128)S(1)}, s32[]{:T(128)}, /*index=5*/s32[64]{0:T(...) while((s32[]{:T(128)}, f32[2,512,128]{2,1,0:T(8,128)}, ...), condition=%wide.region_14.15_spmd.clone, body=%wide.region_10.14_spmd.clone.sunk | while | flops 275760128 | bytes 13450751 | solution.py:138
  570.8 1.9 convolution_add_fusion.2
  576.6 1.9 convolution_add_fusion.2
  582.5 1.9 convolution_add_fusion.2
  594.3 1.9 convolution_add_fusion.2
  612.0 1.9 convolution_add_fusion.2
  629.6 1.9 convolution_add_fusion.2
  647.3 1.9 convolution_add_fusion.2
  665.0 1.9 convolution_add_fusion.2
  682.6 1.9 convolution_add_fusion.2
  700.3 1.9 convolution_add_fusion.2
  718.0 1.9 convolution_add_fusion.2
  732.5 2.0 copy_bitcast_fusion
  (492 shorter events, 178.3 us)
Async XLA Ops:
  6.5 290.8 %copy-start = (bf16[2048,256]{1,0:T(8,128)(2,1)S(1)}, bf16[2048,256]{1,0:T(8,128)(2,1)}, u32[]{:S(2)}) copy-start(bf16[2048,256]{1,0:T(8,128)(2,1)} %param.21) | copy-start | bytes 3145732
  26.6 22.4 %all-to-all-start = ((bf16[32,3,64]{2,1,0:T(4,128)(2,1)}), bf16[32,3,64]{2,1,0:T(4,128)(2,1)S(1)}, u32[]{:S(2)}, u32[]{:S(2)}) async-start(bf16[32,3,64]{2,1,0:T(4,128)(2,1)} %bitcast.8), calls=%async_computation | async-start | bytes 65536 | tf_op jit(solution)/shard_map/all_to_all | solution.py:89
  49.0 100.9 %all-to-all-start.1 = ((bf16[32,64,1024]{2,1,0:T(8,128)(2,1)}), bf16[32,64,1024]{2,1,0:T(8,128)(2,1)}, u32[]{:S(2)}, u32[]{:S(2)}) async-start(bf16[32,64,1024]{2,1,0:T(8,128)(2,1)} %bitcast.64), calls=%async_computation.1 | async-start | bytes 8388608 | tf_op jit(solution)/shard_map/all_to_all | solution.py:88
  56.8 163.2 %all-reduce.2.cloned.1.call-start = ((), (), s32[]{:S(2)}) async-start(), calls=%async_computation.3 | async-start | bytes 4194304 | tf_op jit(solution)/shard_map/psum | solution.py:99
  155.7 74.2 %copy-start.5 = (f32[1024]{0:T(1024)S(1)}, f32[1024]{0:T(1024)}, u32[]{:S(2)}) copy-start(f32[1024]{0:T(1024)} %param.18) | copy-start | bytes 12292
  155.8 141.6 %all-gather.3.cloned.1.call-start = ((), (), s32[]{:S(2)}) async-start(), calls=%async_computation.4 | async-start | bytes 3145728 | tf_op jit(solution)/shard_map/all_gather | solution.py:106
  220.0 9.9 %copy-start.1 = (f32[512,1024]{1,0:T(8,128)S(1)}, f32[512,1024]{1,0:T(8,128)}, u32[]{:S(2)}) copy-start(f32[512,1024]{1,0:T(8,128)} %all-reduce.2.cloned.1.call-done) | copy-start | bytes 6291460
  305.1 5.6 copy-start.6
  305.1 231.4 %all-to-all-start.2 = ((bf16[32,512,2,128]{3,1,2,0:T(8,128)(2,1)}), bf16[32,512,2,128]{3,1,2,0:T(8,128)(2,1)}, u32[]{:S(2)}, u32[]{:S(2)}) async-start(bf16[32,512,2,128]{3,1,2,0:T(8,128)(2,1)} %stack.9), calls=%async_computation.2 | async-start | bytes 16777216 | tf_op jit(solution)/shard_map/all_to_all | solution.py:121
  310.6 233.4 %all-gather.5.cloned.1.call-start = ((), (), s32[]{:S(2)}) async-start(), calls=%async_computation.5 | async-start | bytes 8650752 | tf_op jit(solution)/shard_map/all_gather | solution.py:119
  316.4 227.7 %copy-start.4 = (s32[64]{0:T(128)S(1)}, s32[64]{0:T(128)}, u32[]{:S(2)}) copy-start(s32[64]{0:T(128)} %param.17) | copy-start | bytes 772
  546.2 1.0 copy-start.2
  552.0 1.0 copy-start.2
  557.9 1.0 copy-start.2
  563.8 1.0 copy-start.2
  569.7 1.0 copy-start.2
  581.5 1.0 copy-start.2
  593.3 1.0 copy-start.2
  599.2 1.0 copy-start.2
  605.0 1.0 copy-start.2
  628.6 1.0 copy-start.2
  634.5 1.0 copy-start.2
  640.4 1.0 copy-start.2
  646.3 1.0 copy-start.2
  658.0 1.0 copy-start.2
  669.8 1.0 copy-start.2
  681.6 1.0 copy-start.2
  693.4 1.0 copy-start.2
  705.2 1.0 copy-start.2
  716.9 1.0 copy-start.2
  722.8 1.0 copy-start.2
  728.7 1.0 copy-start.2
  (43 other events, 38.6 us)
Sparse Core Ops, SparseCore 0:
  155.9 64.0 all-reduce.1
  231.3 66.0 all-gather.2
  313.7 184.5 all-gather.4
